TPU v7x, 32 devices: a whole 2x2x4 slice. The times are simulated.
32 devices in a mesh: grp: 2 (over x), row: 16 (over z, y, core).
Axes of the slice: x: 2, y: 2, z: 4, core: 2. Of those that a mesh axis runs over, the one named last changes fastest.
Arguments:
- aligned_sequences: bfloat16 [32, 64, 64], P(None, ('grp', 'row')), parts along dimension 1, may hold values from -6 to 6
- first_factor_matrix: bfloat16 [64, 32], replicated, may hold values from -0.75 to 0.75
- second_factor_matrix: bfloat16 [64, 32], replicated, may hold values from -0.75 to 0.75
- tensor_matrix: bfloat16 [1024, 128], replicated, may hold values from -1 to 1
- tensor_offset: bfloat16 [128], replicated, may hold values from -4 to 4
- structural_duplex_patches: bfloat16 [512, 2048], P(('grp', 'row')), parts along dimension 0, may hold values from -6 to 6
- patch_source_index: int32 [512, 1], P(('grp', 'row')), parts along dimension 0, may hold values from 0 to 15; in each aligned block of 16 rows (0 to 15, 16 to 31, ...) at most 2 rows name the same one
- patch_target_index: int32 [512], P(('grp', 'row')), parts along dimension 0, may hold values from 0 to 1
- structural_matrix: bfloat16 [64, 128], replicated, may hold values from -0.75 to 0.75
- polymer_residue_lengths: int32 [16], P('grp'), parts along dimension 0, may hold values from 1 to 16, 32 in all
- sigmoid_matrix: bfloat16 [128, 128], replicated, may hold values from -0.5 to 0.5
- content_matrix: bfloat16 [128, 128], replicated, may hold values from -0.5 to 0.5
Outputs:
- update: bfloat16 [64, 32, 128], P(('grp', 'row')), parts along dimension 0
There are 2 independent parts, one for each index of `grp`. A program takes and returns all parts, laid end to end along the dimension named above; an argument that names none is the same for every part. Nothing has to cross between parts.
Inputs may be any that keep to these rules, and one draw needn't show every extreme that they name: `patch_source_index`: among the tiles of one device no owner is named more than 2 times, a bound that some block reaches.
All inputs are finite; a program needn't handle non-finite values.
Results may differ from a plain program's by a relative error of at most 0.0073.
Values may be sent and summed in bfloat16 or wider, within the bound.
No kernel may reach another device: no remote copies, remote signals or barrier semaphores. Data moves between devices by JAX's collectives and lax.ppermute only.
A program may use at most 64 MiB of HBM per device.

v0:
```python
import jax
import jax.numpy as jnp
from jax import lax
from jax.sharding import PartitionSpec as P

TC = 16
CAP = 2


def standardize_features(inputs):
    centred = inputs - jnp.mean(inputs, axis=-1, keepdims=True)
    variance = jnp.mean(centred * centred, axis=-1, keepdims=True)
    return centred * lax.rsqrt(variance + 1e-05)


def outer_block(left_mat, right_block, tensor_matrix, tensor_offset, line_total):
    alignment_depth, n_cols, n_chan = right_block.shape
    product = jnp.dot(
        left_mat,
        right_block.reshape(alignment_depth, n_cols * n_chan),
        preferred_element_type=jnp.float32,
    )
    product = (product / alignment_depth).astype(jnp.bfloat16)
    product = (
        product.reshape(line_total, n_chan, n_cols, n_chan)
        .transpose(0, 2, 1, 3)
        .reshape(line_total * n_cols, n_chan * n_chan)
    )
    projected = jnp.dot(
        product, tensor_matrix, preferred_element_type=jnp.float32
    ) + tensor_offset.astype(jnp.float32)
    return projected.reshape(line_total, n_cols, tensor_matrix.shape[1])


def outer_rows(left_mat, right_piece, tensor_matrix, tensor_offset, line_total):
    alignment_depth, n_cols, n_chan = right_piece.shape
    width = 128 if n_cols % 128 == 0 else n_cols
    n_blocks = n_cols // width
    blocks = right_piece.reshape(alignment_depth, n_blocks, width, n_chan).transpose(1, 0, 2, 3)

    def one_block(right_block):
        return outer_block(left_mat, right_block, tensor_matrix, tensor_offset, line_total)

    results = lax.map(one_block, blocks)
    return results.transpose(1, 0, 2, 3).reshape(line_total, n_cols, tensor_matrix.shape[1])


def on_device(
    aligned_sequences,
    first_factor_matrix,
    second_factor_matrix,
    tensor_matrix,
    tensor_offset,
    structural_duplex_patches,
    patch_source_index,
    patch_target_index,
    structural_matrix,
    polymer_residue_lengths,
    sigmoid_matrix,
    content_matrix,
):
    n_devices = lax.axis_size("row")
    device_id = lax.axis_index("row")
    alignment_depth, line_total, discarded_entry = aligned_sequences.shape
    tile_width = structural_duplex_patches.shape[1]
    n_tokens = line_total * n_devices
    n_tiles = n_tokens // TC
    n_chan = first_factor_matrix.shape[1]
    n_temp = structural_matrix.shape[0]
    standardized_features = standardize_features(aligned_sequences.astype(jnp.float32)).astype(
        jnp.bfloat16
    )
    left_side = jnp.dot(
        standardized_features, first_factor_matrix, preferred_element_type=jnp.float32
    ).astype(jnp.bfloat16)
    left_mat = left_side.transpose(1, 2, 0).reshape(line_total * n_chan, alignment_depth)
    second_factor = jnp.dot(
        standardized_features, second_factor_matrix, preferred_element_type=jnp.float32
    ).astype(jnp.bfloat16)
    outer_sum = outer_rows(
        left_mat,
        lax.all_gather(second_factor, "row", axis=1, tiled=True),
        tensor_matrix,
        tensor_offset,
        line_total,
    )
    owners = patch_source_index[:, 0]
    matches = (owners[:, None] == jnp.arange(n_devices, dtype=jnp.int32)[None, :]).astype(jnp.int32)
    ranking = jnp.sum(jnp.cumsum(matches, axis=0) * matches, axis=1) - 1
    target = owners * CAP + ranking
    placing = (target[None, :] == jnp.arange(n_devices * CAP, dtype=jnp.int32)[:, None]).astype(
        jnp.bfloat16
    )
    send_tiles = jnp.dot(
        placing, structural_duplex_patches, preferred_element_type=jnp.float32
    ).astype(jnp.bfloat16)
    send_tiles = send_tiles.reshape(n_devices, CAP, tile_width)
    column_code = (patch_target_index + 1).astype(jnp.float32).astype(jnp.bfloat16)
    send_codes = jnp.dot(placing, column_code[:, None], preferred_element_type=jnp.float32)[:, 0]
    send_codes = send_codes.astype(jnp.bfloat16).reshape(n_devices, CAP)
    got_tiles, got_codes = (
        lax.all_to_all(send_tiles, "row", split_axis=0, concat_axis=0, tiled=True),
        lax.all_to_all(send_codes, "row", split_axis=0, concat_axis=0, tiled=True),
    )
    got_tiles = got_tiles.reshape(n_devices * CAP, tile_width)
    got_codes = got_codes.reshape(n_devices * CAP).astype(jnp.float32)
    tile_ids = (jnp.arange(n_tiles, dtype=jnp.int32) + 1).astype(jnp.float32)
    landing = (got_codes[None, :] == tile_ids[:, None]).astype(jnp.bfloat16)
    tile_sum = jnp.dot(landing, got_tiles, preferred_element_type=jnp.float32)
    tile_count = jnp.sum(landing.astype(jnp.float32), axis=1)
    tile_mean = tile_sum / jnp.maximum(tile_count, 1.0)[:, None]
    tile_mean = (
        tile_mean.reshape(n_tiles, line_total, TC, n_temp)
        .transpose(1, 0, 2, 3)
        .reshape(line_total, n_tokens, n_temp)
    )
    chain_ends = jnp.cumsum(polymer_residue_lengths)
    positions = jnp.arange(n_tokens, dtype=jnp.int32)
    chain_of = jnp.sum((positions[:, None] >= chain_ends[None, :]).astype(jnp.int32), axis=1)
    row_chain = lax.dynamic_slice_in_dim(chain_of, device_id * line_total, line_total)
    same_chain = (row_chain[:, None] == chain_of[None, :]).astype(jnp.float32)
    template_in = (tile_mean * same_chain[:, :, None]).astype(jnp.bfloat16)
    template_pair = jnp.dot(
        template_in.reshape(line_total * n_tokens, n_temp),
        structural_matrix,
        preferred_element_type=jnp.float32,
    )
    pair = template_pair.reshape(line_total, n_tokens, -1) + outer_sum
    pair_normed = standardize_features(pair).astype(jnp.bfloat16).reshape(line_total * n_tokens, -1)
    gating = jax.nn.sigmoid(
        jnp.dot(pair_normed, sigmoid_matrix, preferred_element_type=jnp.float32)
    )
    linear = jnp.dot(pair_normed, content_matrix, preferred_element_type=jnp.float32)
    return (gating * linear).astype(jnp.bfloat16).reshape(line_total, n_tokens, -1)


def solution(mesh):
    placed = (
        P(None, ("grp", "row"), None),
        P(),
        P(),
        P(),
        P(),
        P(("grp", "row"), None),
        P(("grp", "row"), None),
        P(("grp", "row")),
        P(),
        P("grp"),
        P(),
        P(),
    )
    return jax.shard_map(
        on_device,
        mesh=mesh,
        in_specs=placed,
        out_specs=P(("grp", "row"), None, None),
        check_vma=False,
    )
```

profile of v0, /device:TPU:0, one launch (start us, length us, event | category | flops | bytes accessed | tf_op | source)
XLA Modules:
  0.0 53.7 jit_solution(5722045091551390753)
XLA Ops:
  0.0 0.7 %copy-done.7 = s32[16,1]{0,1:T(1,128)S(1)} copy-done((s32[16,1]{0,1:T(1,128)S(1)}, s32[16,1]{0,1:T(1,128)}, u32[]{:S(2)}) %copy-start.7) | copy-done | bytes 88
  0.7 0.1 fusion.19
  0.8 0.2 select_reduce_fusion
  1.0 0.6 %copy-done.9 = s32[16]{0:T(128)S(1)} copy-done((s32[16]{0:T(128)S(1)}, s32[16]{0:T(128)}, u32[]{:S(2)}) %copy-start.9) | copy-done | bytes 88
  1.7 0.1 fusion.6
  1.8 0.7 %convert_element_type.119 = bf16[16,1,2]{2,1,0:T(2,128)(2,1)} reshape(bf16[32]{0:T(256)(128)(2,1)S(1)} %fusion.6) | data formatting | bytes 128 | tf_op jit(solution)/shard_map/convert_element_type | solution.py:100
  2.5 7.4 %all-to-all-start = ((bf16[16,1,2]{2,1,0:T(2,128)(2,1)}), bf16[16,1,2]{2,1,0:T(2,128)(2,1)S(1)}, u32[]{:S(2)}, u32[]{:S(2)}) async-start(bf16[16,1,2]{2,1,0:T(2,128)(2,1)} %convert_element_type.119), calls=%async_computation | async-start | bytes 16384 | tf_op jit(solution)/shard_map/all_to_all | solution.py:103
  9.9 0.1 convert_reduce_fusion
  10.1 0.2 fusion.9
  10.3 0.1 fusion.10
  10.4 0.6 %copy-done.5 = bf16[64,32]{0,1:T(8,128)(2,1)S(1)} copy-done((bf16[64,32]{0,1:T(8,128)(2,1)S(1)}, bf16[64,32]{0,1:T(8,128)(2,1)}, u32[]{:S(2)}) %copy-start.5) | copy-done | bytes 4120
  11.0 0.1 fusion.5
  11.1 0.1 reshape.180
  11.2 0.6 %copy-done.6 = bf16[64,32]{0,1:T(8,128)(2,1)S(1)} copy-done((bf16[64,32]{0,1:T(8,128)(2,1)S(1)}, bf16[64,32]{0,1:T(8,128)(2,1)}, u32[]{:S(2)}) %copy-start.6) | copy-done | bytes 4120
  11.8 0.1 convolution_convert_fusion.1
  11.9 22.4 %all_gather.3 = bf16[32,32,32]{2,0,1:T(8,128)(2,1)S(1)} all-gather(bf16[32,2,32]{2,0,1:T(8,128)(2,1)S(1)} %convolution_convert_fusion.1), channel_id=1, replica_groups=mesh['grp'=2,'row'=16] {'row'}, dimensions={1}, use_global_device_ids=true | all-gather | bytes 69632 | tf_op jit(solution)/shard_map/all_gather | solution.py:82
  34.3 0.1 copy.34
  34.4 0.3 reshape.181
  34.7 0.2 fusion
  34.9 0.4 reshape.182
  35.3 0.2 copy.41
  35.5 0.5 reshape.183
  36.1 0.1 copy-done.10
  36.2 0.2 copy-done.2
  36.4 0.2 convolution_convert_fusion
  36.5 0.6 %copy-done.11 = s32[8]{0:T(128)S(1)} copy-done((s32[8]{0:T(128)S(1)}, s32[8]{0:T(128)}, u32[]{:S(2)}) %copy-start.11) | copy-done | bytes 56
  37.2 0.2 reduce-window.8
  37.4 0.1 convert_reduce_fusion.2
  37.5 0.1 dynamic_slice.6
  37.5 0.1 compare_convert_fusion.1
  37.6 0.2 convolution_add_fusion.1
  37.8 0.7 %reshape.174 = bf16[16,2,2048]{2,1,0:T(2,128)(2,1)} reshape(bf16[32,2048]{1,0:T(8,128)(2,1)S(1)} %convolution_convert_fusion) | data formatting | bytes 262144 | tf_op jit(solution)/shard_map/reshape | solution.py:97
  38.6 3.5 %all-to-all-start.1 = ((bf16[16,2,2048]{2,1,0:T(2,128)(2,1)}), bf16[16,2,2048]{2,1,0:T(2,128)(2,1)S(1)}, u32[]{:S(2)}, u32[]{:S(2)}) async-start(bf16[16,2,2048]{2,1,0:T(2,128)(2,1)} %reshape.174), calls=%async_computation.1 | async-start | bytes 262144 | tf_op jit(solution)/shard_map/all_to_all | solution.py:102
  42.1 0.1 reshape.186
  42.2 0.2 convert_reduce_fusion.3
  42.4 7.6 %all-to-all-done.1 = bf16[16,2,2048]{2,1,0:T(2,128)(2,1)S(1)} async-done(((bf16[16,2,2048]{2,1,0:T(2,128)(2,1)}), bf16[16,2,2048]{2,1,0:T(2,128)(2,1)S(1)}, u32[]{:S(2)}, u32[]{:S(2)}) %all-to-all-start.1) | async-done | bytes 131104 | tf_op jit(solution)/shard_map/all_to_all | solution.py:102
  49.9 0.1 reshape.175
  50.0 0.2 convolution_divide_fusion
  50.2 0.1 reshape.176
  50.3 0.1 fusion.11
  50.4 0.6 %copy-done.4 = bf16[64,128]{1,0:T(8,128)(2,1)S(1)} copy-done((bf16[64,128]{1,0:T(8,128)(2,1)S(1)}, bf16[64,128]{1,0:T(8,128)(2,1)}, u32[]{:S(2)}) %copy-start.4) | copy-done | bytes 16408
  51.0 0.2 fusion.27
  51.2 0.2 multiply_reduce_fusion
  51.4 0.1 multiply_convert_fusion
  51.5 0.7 %copy-done.8 = bf16[128,128]{1,0:T(8,128)(2,1)S(1)} copy-done((bf16[128,128]{1,0:T(8,128)(2,1)S(1)}, bf16[128,128]{1,0:T(8,128)(2,1)}, u32[]{:S(2)}) %copy-start.8) | copy-done | bytes 32792
  52.2 0.1 fusion.3
  52.3 0.6 %copy-done.3 = bf16[128,128]{1,0:T(8,128)(2,1)S(1)} copy-done((bf16[128,128]{1,0:T(8,128)(2,1)S(1)}, bf16[128,128]{1,0:T(8,128)(2,1)}, u32[]{:S(2)}) %copy-start.3) | copy-done | bytes 32792
  52.9 0.7 %fusion.4 = bf16[64,128]{1,0:T(8,128)(2,1)} fusion(f32[64,128]{1,0:T(8,128)S(1)} %fusion.3, bf16[64,128]{1,0:T(8,128)(2,1)S(1)} %bitcast.54, bf16[128,128]{1,0:T(8,128)(2,1)S(1)} %copy-done.3), kind=kOutput, calls=%fused_computation.11 | convolution fusion | flops 2113536 | bytes 98304 | tf_op jit(solution)/shard_map/dot_general | solution.py:133
  (27 shorter events, 0.2 us)
Async XLA Ops:
  0.0 37.6 %copy-start = (bf16[1024,128]{1,0:T(8,128)(2,1)S(1)}, bf16[1024,128]{1,0:T(8,128)(2,1)}, u32[]{:S(2)}) copy-start(bf16[1024,128]{1,0:T(8,128)(2,1)} %param.15) | copy-start | bytes 786436
  0.0 0.7 %copy-start.7 = (s32[16,1]{0,1:T(1,128)S(1)}, s32[16,1]{0,1:T(1,128)}, u32[]{:S(2)}) copy-start(s32[16,1]{0,1:T(1,128)} %param.18) | copy-start | bytes 196
  1.0 0.7 %copy-start.9 = (s32[16]{0:T(128)S(1)}, s32[16]{0:T(128)}, u32[]{:S(2)}) copy-start(s32[16]{0:T(128)} %param.19) | copy-start | bytes 196
  1.7 8.3 %copy-start.1 = (bf16[32,2,64]{2,1,0:T(2,128)(2,1)S(1)}, bf16[32,2,64]{2,1,0:T(2,128)(2,1)}, u32[]{:S(2)}) copy-start(bf16[32,2,64]{2,1,0:T(2,128)(2,1)} %param.12) | copy-start | bytes 24580
  2.5 36.1 %all-to-all-start = ((bf16[16,1,2]{2,1,0:T(2,128)(2,1)}), bf16[16,1,2]{2,1,0:T(2,128)(2,1)S(1)}, u32[]{:S(2)}, u32[]{:S(2)}) async-start(bf16[16,1,2]{2,1,0:T(2,128)(2,1)} %convert_element_type.119), calls=%async_computation | async-start | bytes 16384 | tf_op jit(solution)/shard_map/all_to_all | solution.py:103
  10.3 0.7 %copy-start.5 = (bf16[64,32]{0,1:T(8,128)(2,1)S(1)}, bf16[64,32]{0,1:T(8,128)(2,1)}, u32[]{:S(2)}) copy-start(bf16[64,32]{0,1:T(8,128)(2,1)} %param.13) | copy-start | bytes 12292
  11.1 0.7 %copy-start.6 = (bf16[64,32]{0,1:T(8,128)(2,1)S(1)}, bf16[64,32]{0,1:T(8,128)(2,1)}, u32[]{:S(2)}) copy-start(bf16[64,32]{0,1:T(8,128)(2,1)} %param.14) | copy-start | bytes 12292
  35.5 0.7 %copy-start.10 = (bf16[128]{0:T(256)(128)(2,1)S(1)}, bf16[128]{0:T(256)(128)(2,1)}, u32[]{:S(2)}) copy-start(bf16[128]{0:T(256)(128)(2,1)} %param.16) | copy-start | bytes 772
  35.5 0.8 %copy-start.2 = (bf16[16,2048]{1,0:T(8,128)(2,1)S(1)}, bf16[16,2048]{1,0:T(8,128)(2,1)}, u32[]{:S(2)}) copy-start(bf16[16,2048]{1,0:T(8,128)(2,1)} %param.17) | copy-start | bytes 196612
  36.5 0.7 %copy-start.11 = (s32[8]{0:T(128)S(1)}, s32[8]{0:T(128)}, u32[]{:S(2)}) copy-start(s32[8]{0:T(128)} %param.21) | copy-start | bytes 100
  38.6 11.4 %all-to-all-start.1 = ((bf16[16,2,2048]{2,1,0:T(2,128)(2,1)}), bf16[16,2,2048]{2,1,0:T(2,128)(2,1)S(1)}, u32[]{:S(2)}, u32[]{:S(2)}) async-start(bf16[16,2,2048]{2,1,0:T(2,128)(2,1)} %reshape.174), calls=%async_computation.1 | async-start | bytes 262144 | tf_op jit(solution)/shard_map/all_to_all | solution.py:102
  50.3 0.7 %copy-start.4 = (bf16[64,128]{1,0:T(8,128)(2,1)S(1)}, bf16[64,128]{1,0:T(8,128)(2,1)}, u32[]{:S(2)}) copy-start(bf16[64,128]{1,0:T(8,128)(2,1)} %param.20) | copy-start | bytes 49156
  51.4 0.8 %copy-start.8 = (bf16[128,128]{1,0:T(8,128)(2,1)S(1)}, bf16[128,128]{1,0:T(8,128)(2,1)}, u32[]{:S(2)}) copy-start(bf16[128,128]{1,0:T(8,128)(2,1)} %param.22) | copy-start | bytes 98308
  52.2 0.8 %copy-start.3 = (bf16[128,128]{1,0:T(8,128)(2,1)S(1)}, bf16[128,128]{1,0:T(8,128)(2,1)}, u32[]{:S(2)}) copy-start(bf16[128,128]{1,0:T(8,128)(2,1)} %param.23) | copy-start | bytes 98308
where the time goes:
time: 54.3 us; the launch traced here: 53.7 us
  blocking collectives  22.4 us (41%)
  starting transfers between devices  10.9 us (20%)
  local copies, waits for them, and re-layouts  8.71 us (16%)
  waiting for transfers between devices  7.56 us (14%)
  matrix products  2.18 us (4%)
  other arithmetic  1.63 us (3%)
    all_gather x1, blocking collectives, on_device(): lax.all_gather(second_factor, 'row', axis=1, tiled=True)  22.4 us
    all_to_all x1, waiting for transfers between devices, on_device(): lax.all_to_all(send_tiles, 'row', split_axis=0, concat_axis=0, tiled=True)  7.56 us
    all_to_all x1, starting transfers between devices, on_device(): lax.all_to_all(send_codes, 'row', split_axis=0, concat_axis=0, tiled=True)  7.41 us
    unnamed x24, local copies, waits for them, and re-layouts  5.37 us
    all_to_all x1, starting transfers between devices, on_device(): lax.all_to_all(send_tiles, 'row', split_axis=0, concat_axis=0, tiled=True)  3.51 us
  transfers between devices with their start and end apart: 2, of which 1 were waited for; matrix products, arithmetic and copies ran while one was open for 8% of the time, Pallas kernels for 0%

commit v1 on v0

v1 whole, which is shorter than its diff:
```python
import functools

import jax
import jax.numpy as jnp
from jax import lax
from jax.experimental import pallas as pl
from jax.experimental.pallas import tpu as pltpu
from jax.sharding import PartitionSpec as P

CAP = 2
LANES = 128
CODE_ROWS = 8
VMEM = pltpu.MemorySpace.VMEM
SMEM = pltpu.MemorySpace.SMEM


def dot(a, b):
    return jnp.dot(a, b, preferred_element_type=jnp.float32)


def dot_nt(a, b):
    return lax.dot_general(a, b, (((1,), (1,)), ((), ())), preferred_element_type=jnp.float32)


def standardize(x):
    centred = x - jnp.mean(x, axis=-1, keepdims=True)
    variance = jnp.mean(centred * centred, axis=-1, keepdims=True)
    return centred * lax.rsqrt(variance + 1e-05)


def pack_kernel(n_devices, rows, x_ref, second_ref, tiles_ref, owner_ref, column_ref, send_ref, normed_ref, wide):
    depth, lines, _ = x_ref.shape
    slots, width = tiles_ref.shape
    tile_rows = width // LANES
    n_chan = second_ref.shape[0]
    right_rows = n_chan * depth // LANES
    x = x_ref[...].astype(jnp.float32)
    for t in range(lines):
        normed = standardize(x[:, t, :]).astype(jnp.bfloat16)
        normed_ref[pl.ds(t * depth, depth), :] = normed
        right = dot_nt(second_ref[...], normed)
        groups = n_chan // right_rows
        packed = jnp.concatenate(
            [right[b * right_rows : (b + 1) * right_rows] for b in range(groups)], axis=1
        )
        for d in range(n_devices):
            wide[pl.ds(d * rows + t * right_rows, right_rows), :] = packed
    owner = owner_ref[...]
    here = lax.broadcasted_iota(jnp.int32, (slots, slots), 0)
    there = lax.broadcasted_iota(jnp.int32, (slots, slots), 1)
    across = jnp.broadcast_to(owner, (slots, slots))
    down = jnp.sum(jnp.where(here == there, across, 0), axis=1, keepdims=True)
    rank = jnp.sum(jnp.where((down == across) & (here < there), 1, 0), axis=0, keepdims=True)
    target = rank * n_devices + owner
    place = lax.broadcasted_iota(jnp.int32, (CAP * n_devices, slots), 0) == target
    base = lines * right_rows
    code = jnp.where(place, (column_ref[...] + 1).astype(jnp.float32), 0.0)
    code = jnp.sum(code, axis=1, keepdims=True)
    code = jnp.broadcast_to(code, (CAP * n_devices, LANES))
    place = place.astype(jnp.bfloat16)
    for q in range(tile_rows):
        placed = dot(place, tiles_ref[:, q * LANES : (q + 1) * LANES])
        for c in range(CAP):
            wide[pl.ds(base + c * tile_rows + q, n_devices, stride=rows), :] = placed[
                c * n_devices : (c + 1) * n_devices
            ]
    base = base + CAP * tile_rows
    for c in range(CODE_ROWS):
        piece = min(c, CAP - 1)
        wide[pl.ds(base + c, n_devices, stride=rows), :] = code[piece * n_devices : (piece + 1) * n_devices]
    send_ref[...] = wide[...].astype(jnp.bfloat16)


def left_kernel(
    n_tiles, tc, normed_ref, first_ref, tensor_ref, lengths_ref, device_ref, folded_ref, same_ref
):
    n_chan = first_ref.shape[0]
    pair_chan = tensor_ref.shape[2]
    lines = folded_ref.shape[1] // pair_chan
    depth = normed_ref.shape[0] // lines
    left = dot_nt(normed_ref[...], first_ref[...]).astype(jnp.bfloat16)
    right_rows = n_chan * depth // LANES
    groups = n_chan // right_rows
    for d in range(n_chan):
        part = (dot(left, tensor_ref[d]) / depth).astype(jnp.bfloat16)
        at = (d % right_rows) * LANES + (d // right_rows) * depth
        for t in range(lines):
            folded_ref[pl.ds(at, depth), t * pair_chan : (t + 1) * pair_chan] = part[
                t * depth : (t + 1) * depth
            ]
    height, _ = same_ref.shape
    tile_rows = height // n_tiles
    per_row = tile_rows // lines
    packed = tc // per_row
    row = lax.broadcasted_iota(jnp.int32, same_ref.shape, 0)
    lane = lax.broadcasted_iota(jnp.int32, same_ref.shape, 1)
    column = (row // tile_rows) * tc + (row % per_row) * packed + lane // (LANES // packed)
    line = device_ref[0] * lines + (row % tile_rows) // per_row
    end = jnp.int32(0)
    column_chain = jnp.zeros_like(column)
    line_chain = jnp.zeros_like(line)
    for c in range(lengths_ref.shape[0]):
        end = end + lengths_ref[c]
        column_chain = column_chain + (column >= end).astype(jnp.int32)
        line_chain = line_chain + (line >= end).astype(jnp.int32)
    same_ref[...] = (column_chain == line_chain).astype(jnp.float32)


def pair_kernel(
    n_devices,
    rows,
    tc,
    got_ref,
    folded_ref,
    same_ref,
    offset_ref,
    structural_ref,
    sigmoid_ref,
    content_ref,
    out_ref,
    right_wide,
    sums,
    pair,
):
    n_temp, pair_chan = structural_ref.shape
    lines = folded_ref.shape[1] // pair_chan
    depth_chan = folded_ref.shape[0]
    right_rows = depth_chan // LANES
    n_tokens = n_devices * lines
    height = same_ref.shape[0]
    n_tiles = n_tokens // tc
    tile_rows = height // n_tiles
    base = lines * right_rows
    code_base = base + CAP * tile_rows

    sums[...] = jnp.zeros_like(sums)

    def add_source(d, carry):
        start = pl.multiple_of(d * rows, 8)
        right_wide[pl.ds(pl.multiple_of(d * base, 8), base), :] = got_ref[pl.ds(start, base), :].astype(
            jnp.float32
        )
        codes = got_ref[pl.ds(start + code_base, CODE_ROWS), :].astype(jnp.float32)
        counts = list(carry)
        for c in range(CAP):
            tile = got_ref[pl.ds(start + base + c * tile_rows, tile_rows), :].astype(jnp.float32)
            code = codes[c : c + 1, :]
            for k in range(n_tiles):
                hit = code == k + 1.0
                counts[k] = counts[k] + jnp.where(hit, 1.0, 0.0)
                at = pl.ds(k * tile_rows, tile_rows)
                sums[at, :] = sums[at, :] + jnp.where(hit, tile, 0.0)
        return tuple(counts)

    counts = tuple(jnp.zeros((1, LANES), jnp.float32) for _ in range(n_tiles))
    counts = lax.fori_loop(0, n_devices, add_source, counts, unroll=n_devices <= 16)
    for k in range(n_tiles):
        at = pl.ds(k * tile_rows, tile_rows)
        mean = sums[at, :] / jnp.maximum(counts[k], 1.0)
        template = (mean * same_ref[at, :]).astype(jnp.bfloat16)
        for h in range(LANES // n_temp):
            part = dot(template[:, h * n_temp : (h + 1) * n_temp], structural_ref[...])
            per_row = tile_rows // lines
            for t in range(lines):
                pair[pl.ds(t * n_tokens + k * tc + h, per_row, stride=LANES // n_temp), :] = part[
                    t * per_row : (t + 1) * per_row
                ]
    outer = None
    for g in range(right_rows):
        lhs = right_wide[pl.ds(g, n_tokens, stride=right_rows), :].astype(jnp.bfloat16)
        term = dot(lhs, folded_ref[pl.ds(g * LANES, LANES), :])
        outer = term if outer is None else outer + term
    for t in range(lines):
        at = pl.ds(t * n_tokens, n_tokens)
        total = pair[at, :] + (outer[:, t * pair_chan : (t + 1) * pair_chan] + offset_ref[...])
        pair_normed = standardize(total).astype(jnp.bfloat16)
        gate = jax.nn.sigmoid(dot(pair_normed, sigmoid_ref[...]))
        linear = dot(pair_normed, content_ref[...])
        out_ref[at, :] = (gate * linear).astype(out_ref.dtype)


def on_device(
    aligned_sequences,
    first_factor_matrix,
    second_factor_matrix,
    tensor_matrix,
    tensor_offset,
    structural_duplex_patches,
    patch_source_index,
    patch_target_index,
    structural_matrix,
    polymer_residue_lengths,
    sigmoid_matrix,
    content_matrix,
):
    n_devices = lax.axis_size("row")
    device_id = lax.axis_index("row")
    depth, lines, n_feat = aligned_sequences.shape
    slots, width = structural_duplex_patches.shape
    n_chan = first_factor_matrix.shape[1]
    n_temp, pair_chan = structural_matrix.shape
    tc = width // (lines * n_temp)
    n_tokens = lines * n_devices
    n_tiles = n_tokens // tc
    tile_rows = width // LANES
    right_rows = n_chan * depth // LANES
    rows = lines * right_rows + CAP * tile_rows + CODE_ROWS
    vmem = pl.BlockSpec(memory_space=VMEM)
    smem = pl.BlockSpec(memory_space=SMEM)

    send, normed = pl.pallas_call(
        functools.partial(pack_kernel, n_devices, rows),
        out_shape=(
            jax.ShapeDtypeStruct((n_devices * rows, LANES), jnp.bfloat16),
            jax.ShapeDtypeStruct((lines * depth, n_feat), jnp.bfloat16),
        ),
        in_specs=[vmem] * 5,
        out_specs=(vmem, vmem),
        scratch_shapes=[pltpu.VMEM((n_devices * rows, LANES), jnp.float32)],
    )(
        aligned_sequences,
        second_factor_matrix.T,
        structural_duplex_patches,
        patch_source_index.reshape(1, slots),
        patch_target_index.reshape(1, slots),
    )
    got = lax.all_to_all(
        send.reshape(n_devices, rows, LANES), "row", split_axis=0, concat_axis=0, tiled=True
    ).reshape(n_devices * rows, LANES)
    folded, same = pl.pallas_call(
        functools.partial(left_kernel, n_tiles, tc),
        out_shape=(
            jax.ShapeDtypeStruct((n_chan * depth, lines * pair_chan), jnp.bfloat16),
            jax.ShapeDtypeStruct((n_tiles * tile_rows, LANES), jnp.float32),
        ),
        in_specs=[vmem] * 3 + [smem] * 2,
        out_specs=(vmem, vmem),
    )(
        normed,
        first_factor_matrix.T,
        tensor_matrix.reshape(n_chan, n_chan, pair_chan).transpose(1, 0, 2),
        polymer_residue_lengths,
        device_id.reshape(1),
    )
    out = pl.pallas_call(
        functools.partial(pair_kernel, n_devices, rows, tc),
        out_shape=jax.ShapeDtypeStruct((lines * n_tokens, pair_chan), jnp.bfloat16),
        in_specs=[vmem] * 7,
        out_specs=vmem,
        scratch_shapes=[
            pltpu.VMEM((n_devices * lines * right_rows, LANES), jnp.float32),
            pltpu.VMEM((n_tiles * tile_rows, LANES), jnp.float32),
            pltpu.VMEM((lines * n_tokens, pair_chan), jnp.float32),
        ],
    )(
        got,
        folded,
        same,
        tensor_offset.astype(jnp.float32).reshape(1, pair_chan),
        structural_matrix,
        sigmoid_matrix,
        content_matrix,
    )
    return out.reshape(lines, n_tokens, pair_chan)


def solution(mesh):
    placed = (
        P(None, ("grp", "row"), None),
        P(),
        P(),
        P(),
        P(),
        P(("grp", "row"), None),
        P(("grp", "row"), None),
        P(("grp", "row")),
        P(),
        P("grp"),
        P(),
        P(),
    )
    return jax.shard_map(
        on_device,
        mesh=mesh,
        in_specs=placed,
        out_specs=P(("grp", "row"), None, None),
        check_vma=False,
    )
```

time: 54.3 us -> 22.3 us (0.41)
  blocking collectives: 22.4 us -> 0 us
  local copies, waits for them, and re-layouts: 8.71 us -> 1.5 us
  Pallas kernels: 0 us -> 6.64 us
  starting transfers between devices: 10.9 us -> 7.41 us
  matrix products: 2.18 us -> 0 us
  waiting for transfers between devices: 7.56 us -> 5.88 us
  other arithmetic: 1.63 us -> 0.57 us
    all_gather x1 -> x0, blocking collectives: 22.4 us -> none  [on_device(): lax.all_gather(second_factor, 'row', axis=1, tiled=True)]
    pallas_call x0 -> x3, Pallas kernels: none -> 6.64 us  [the longest x1 2.39 us: on_device(): pl.pallas_call(functools.partial(pair_kernel, n_devices, rows, tc), out_s...]
    unnamed x24 -> x6, local copies, waits for them, and re-layouts: 5.37 us -> 0.69 us
    all_to_all x2 -> x1, starting transfers between devices: 10.9 us -> 7.41 us  [on_device(): lax.all_to_all(send.reshape(n_devices, rows, LANES), 'row', split_axis=0,...]
    dot_general x10 -> x0, matrix products: 2.18 us -> none  [the longest x1 0.74 us: on_device(): jnp.dot(pair_normed, content_matrix, preferred_element_type=jnp.float32)]
    all_to_all x2 -> x1, waiting for transfers between devices: 7.56 us -> 5.88 us  [on_device(): lax.all_to_all(send.reshape(n_devices, rows, LANES), 'row', split_axis=0,...]
    reshape x8 -> x1, local copies, waits for them, and re-layouts: 2.35 us -> 0.81 us  [on_device(): tensor_matrix.reshape(n_chan, n_chan, pair_chan).transpose(1, 0, 2)]
    reduce_sum x6 -> x0, other arithmetic: 0.9 us -> none  [the longest x2 0.34 us: standardize_features(): variance = jnp.mean(centred * centred, axis=-1, keepdims=True)]
  transfers between devices with their start and end apart: 2 -> 1, of which waited for: 1 -> 1; matrix products, arithmetic and copies ran while one was open for 8% -> 6% of each run, Pallas kernels for 0% -> 10%
where the time goes in v1:
time: 22.3 us; the launch traced here: 22 us
  starting transfers between devices  7.41 us (33%)
  Pallas kernels  6.64 us (30%)
  waiting for transfers between devices  5.88 us (26%)
  local copies, waits for them, and re-layouts  1.5 us (7%)
  other arithmetic  0.57 us (3%)
    all_to_all x1, starting transfers between devices, on_device(): lax.all_to_all(send.reshape(n_devices, rows, LANES), 'row', split_axis=0,...  7.41 us
    all_to_all x1, waiting for transfers between devices, on_device(): lax.all_to_all(send.reshape(n_devices, rows, LANES), 'row', split_axis=0,...  5.88 us
    pallas_call x1, Pallas kernels, on_device(): pl.pallas_call(functools.partial(pair_kernel, n_devices, rows, tc), out_s...  2.39 us
    pallas_call x1, Pallas kernels, on_device(): pl.pallas_call(functools.partial(left_kernel, n_tiles, tc), out_shape=(ja...  2.21 us
    pallas_call x1, Pallas kernels, on_device(): pl.pallas_call(functools.partial(pack_kernel, n_devices, rows), out_shape...  2.03 us
    reshape x1, local copies, waits for them, and re-layouts, on_device(): tensor_matrix.reshape(n_chan, n_chan, pair_chan).transpose(1, 0, 2)  0.81 us
    unnamed x6, local copies, waits for them, and re-layouts  0.69 us
    reshape x1, other arithmetic, on_device(): tensor_offset.astype(jnp.float32).reshape(1, pair_chan)  0.57 us
  transfers between devices with their start and end apart: 1, of which 1 were waited for; matrix products, arithmetic and copies ran while one was open for 6% of the time, Pallas kernels for 10%

profile of v1, /device:TPU:0, one launch (start us, length us, event | category | flops | bytes accessed | tf_op | source)
XLA Modules:
  0.0 22.0 jit_solution(17801728917109413615)
XLA Ops:
  0.0 0.0 copy-start.1
  0.0 2.0 %shard_map.118 = (bf16[896,128]{1,0:T(8,128)(2,1)}, bf16[64,64]{1,0:T(8,128)(2,1)}) custom-call(bf16[32,2,64]{2,1,0:T(2,128)(2,1)} %x_ref.1, bf16[32,64]{1,0:T(8,128)(2,1)} %bitcast.19, bf16[16,2048]{1,0:T(8,128)(2,1)} %tiles_ref.1, s32[1,16]{1,0:T(1,128)} %bitcast.21, s32[1,16]{1,0:T(1,128)} %bitcast.22), custom_call_target="tpu_custom_call" | custom-call | tf_op jit(solution)/shard_map/pallas_call | solution.py:211
  2.0 7.4 %all-to-all-start = ((bf16[16,56,128]{2,1,0:T(8,128)(2,1)}), bf16[16,56,128]{2,1,0:T(8,128)(2,1)S(1)}, u32[]{:S(2)}, u32[]{:S(2)}) async-start(bf16[16,56,128]{2,1,0:T(8,128)(2,1)} %bitcast.18), calls=%async_computation | async-start | bytes 458752 | tf_op jit(solution)/shard_map/all_to_all | solution.py:227
  9.5 0.0 copy-done.1
  9.5 0.8 %copy.15 = bf16[32,32,128]{2,0,1:T(8,128)(2,1)} copy(bf16[32,32,128]{2,1,0:T(8,128)(2,1)S(1)} %bitcast.17) | data formatting | bytes 524288 | tf_op jit(solution)/shard_map/reshape | solution.py:241
  10.3 0.0 copy-start.2
  10.3 2.2 %shard_map.119 = (bf16[1024,256]{1,0:T(8,128)(2,1)}, f32[32,128]{1,0:T(8,128)}) custom-call(bf16[64,64]{1,0:T(8,128)(2,1)} %get-tuple-element.10.normed_ref, bf16[32,64]{1,0:T(8,128)(2,1)} %bitcast.20, bf16[32,32,128]{2,1,0:T(8,128)(2,1)} %bitcast.15, s32[8]{0:T(128)} %lengths_ref.1, s32[1]{0:T(128)} %bitcast.8.device_ref), custom_call_target="tpu_custom_call" | custom-call | tf_op jit(solution)/shard_map/pallas_call | solution.py:230
  12.5 0.0 copy-done.2
  12.5 0.6 %bitcast_convert_fusion.offset_ref = f32[1,128]{1,0:T(1,128)} fusion(bf16[128]{0:T(256)(128)(2,1)S(1)} %copy-done.2), kind=kLoop, calls=%fused_computation.1 | loop fusion | flops 128 | bytes 768 | tf_op jit(solution)/shard_map/reshape | solution.py:259
  13.1 5.9 %all-to-all-done = bf16[16,56,128]{2,1,0:T(8,128)(2,1)S(1)} async-done(((bf16[16,56,128]{2,1,0:T(8,128)(2,1)}), bf16[16,56,128]{2,1,0:T(8,128)(2,1)S(1)}, u32[]{:S(2)}, u32[]{:S(2)}) %all-to-all-start) | async-done | bytes 229408 | tf_op jit(solution)/shard_map/all_to_all | solution.py:227
  18.9 0.0 copy-start
  18.9 0.7 %copy-done = bf16[16,56,128]{2,1,0:T(8,128)(2,1)} copy-done((bf16[16,56,128]{2,1,0:T(8,128)(2,1)}, bf16[16,56,128]{2,1,0:T(8,128)(2,1)S(1)}, u32[]{:S(2)}) %copy-start) | copy-done | bytes 229400
  19.6 2.4 %shard_map.120 = bf16[64,128]{1,0:T(8,128)(2,1)} custom-call(bf16[896,128]{1,0:T(8,128)(2,1)} %bitcast.16, bf16[1024,256]{1,0:T(8,128)(2,1)} %get-tuple-element.11.folded_ref, f32[32,128]{1,0:T(8,128)} %get-tuple-element.12.same_ref, f32[1,128]{1,0:T(1,128)} %bitcast_convert_fusion.offset_ref, bf16[64,128]{1,0:T(8,128)(2,1)} %structural_ref.1, ...), custom_call_target="tpu_custom_call" | custom-call | tf_op jit(solution)/shard_map/pallas_call | solution.py:245
Async XLA Ops:
  0.0 9.5 %copy-start.1 = (bf16[1024,128]{1,0:T(8,128)(2,1)S(1)}, bf16[1024,128]{1,0:T(8,128)(2,1)}, u32[]{:S(2)}) copy-start(bf16[1024,128]{1,0:T(8,128)(2,1)} %param.15) | copy-start | bytes 786436
  2.0 16.9 %all-to-all-start = ((bf16[16,56,128]{2,1,0:T(8,128)(2,1)}), bf16[16,56,128]{2,1,0:T(8,128)(2,1)S(1)}, u32[]{:S(2)}, u32[]{:S(2)}) async-start(bf16[16,56,128]{2,1,0:T(8,128)(2,1)} %bitcast.18), calls=%async_computation | async-start | bytes 458752 | tf_op jit(solution)/shard_map/all_to_all | solution.py:227
  10.3 2.2 %copy-start.2 = (bf16[128]{0:T(256)(128)(2,1)S(1)}, bf16[128]{0:T(256)(128)(2,1)}, u32[]{:S(2)}) copy-start(bf16[128]{0:T(256)(128)(2,1)} %param.16) | copy-start | bytes 772
  18.9 0.7 %copy-start = (bf16[16,56,128]{2,1,0:T(8,128)(2,1)}, bf16[16,56,128]{2,1,0:T(8,128)(2,1)S(1)}, u32[]{:S(2)}) copy-start(bf16[16,56,128]{2,1,0:T(8,128)(2,1)S(1)} %all-to-all-done) | copy-start | bytes 688132

commit v2 on v1

--- a/solution.py
+++ b/solution.py
@@ -1,4 +1,5 @@
 import functools
+import math
 
 import jax
 import jax.numpy as jnp
@@ -179,6 +180,12 @@
         out_ref[at, :] = (gate * linear).astype(out_ref.dtype)
 
 
+def grant(*arrays):
+    return pltpu.CompilerParams(
+        vmem_limit_bytes=sum(2 * math.prod(shape) * jnp.dtype(kind).itemsize for shape, kind in arrays) + (1 << 20)
+    )
+
+
 def on_device(
     aligned_sequences,
     first_factor_matrix,
@@ -235,6 +242,11 @@
         ),
         in_specs=[vmem] * 3 + [smem] * 2,
         out_specs=(vmem, vmem),
+        compiler_params=grant(
+            ((n_chan * n_chan, pair_chan), jnp.bfloat16),
+            ((n_chan * depth, lines * pair_chan), jnp.bfloat16),
+            ((n_tiles * tile_rows, LANES), jnp.float32),
+        ),
     )(
         normed,
         first_factor_matrix.T,
@@ -252,6 +264,13 @@
             pltpu.VMEM((n_tiles * tile_rows, LANES), jnp.float32),
             pltpu.VMEM((lines * n_tokens, pair_chan), jnp.float32),
         ],
+        compiler_params=grant(
+            ((n_devices * rows, LANES), jnp.bfloat16),
+            ((n_chan * depth, lines * pair_chan), jnp.bfloat16),
+            ((n_devices * lines * right_rows, LANES), jnp.float32),
+            ((2 * n_tiles * tile_rows, LANES), jnp.float32),
+            ((2 * lines * n_tokens, pair_chan), jnp.float32),
+        ),
     )(
         got,
         folded,

time: 22.3 us -> 20.6 us (0.924)
  Pallas kernels: 6.64 us -> 4.25 us
  waiting for transfers between devices: 5.88 us -> 7.65 us
  local copies, waits for them, and re-layouts: 1.5 us -> 0.81 us
  other arithmetic: 0.57 us -> 0.01 us
    all_to_all x1, waiting for transfers between devices: 5.88 us -> 7.65 us  [on_device(): lax.all_to_all(send.reshape(n_devices, rows, LANES), 'row', split_axis=0,...]
    pallas_call x1, Pallas kernels: 2.21 us -> 0.94 us  [on_device(): pl.pallas_call(functools.partial(left_kernel, n_tiles, tc), out_shape=(ja...]
    pallas_call x1, Pallas kernels: 2.39 us -> 1.28 us  [on_device(): pl.pallas_call(functools.partial(pair_kernel, n_devices, rows, tc), out_s...]
    reshape x1, local copies, waits for them, and re-layouts: 0.81 us -> 0.11 us  [on_device(): tensor_matrix.reshape(n_chan, n_chan, pair_chan).transpose(1, 0, 2)]
    reshape x1, other arithmetic: 0.57 us -> 0.01 us  [on_device(): tensor_offset.astype(jnp.float32).reshape(1, pair_chan)]
    unnamed x6 -> x16, local copies, waits for them, and re-layouts: 0.69 us -> 0.71 us
  transfers between devices with their start and end apart: 1 -> 1, of which waited for: 1 -> 1; matrix products, arithmetic and copies ran while one was open for 6% -> 1% of each run, Pallas kernels for 10% -> 5%
where the time goes in v2:
time: 20.6 us; the launch traced here: 20.2 us
  waiting for transfers between devices  7.65 us (37%)
  starting transfers between devices  7.41 us (36%)
  Pallas kernels  4.25 us (21%)
  local copies, waits for them, and re-layouts  0.81 us (4%)
    all_to_all x1, waiting for transfers between devices, on_device(): lax.all_to_all(send.reshape(n_devices, rows, LANES), 'row', split_axis=0,...  7.65 us
    all_to_all x1, starting transfers between devices, on_device(): lax.all_to_all(send.reshape(n_devices, rows, LANES), 'row', split_axis=0,...  7.41 us
    pallas_call x1, Pallas kernels, on_device(): pl.pallas_call(functools.partial(pack_kernel, n_devices, rows), out_shape...  2.03 us
    pallas_call x1, Pallas kernels, on_device(): pl.pallas_call(functools.partial(pair_kernel, n_devices, rows, tc), out_s...  1.28 us
    pallas_call x1, Pallas kernels, on_device(): pl.pallas_call(functools.partial(left_kernel, n_tiles, tc), out_shape=(ja...  0.94 us
    unnamed x16, local copies, waits for them, and re-layouts  0.71 us
  transfers between devices with their start and end apart: 1, of which 1 were waited for; matrix products, arithmetic and copies ran while one was open for 1% of the time, Pallas kernels for 5%

profile of v2, /device:TPU:0, one launch (start us, length us, event | category | flops | bytes accessed | tf_op | source)
XLA Modules:
  0.0 20.2 jit_solution(15709043462696596947)
XLA Ops:
  0.0 0.0 copy-start.6
  0.0 2.0 %shard_map.118 = (bf16[896,128]{1,0:T(8,128)(2,1)}, bf16[64,64]{1,0:T(8,128)(2,1)}) custom-call(bf16[32,2,64]{2,1,0:T(2,128)(2,1)} %x_ref.1, bf16[32,64]{1,0:T(8,128)(2,1)} %bitcast.20, bf16[16,2048]{1,0:T(8,128)(2,1)} %tiles_ref.1, s32[1,16]{1,0:T(1,128)} %bitcast.21, s32[1,16]{1,0:T(1,128)} %bitcast.22), custom_call_target="tpu_custom_call" | custom-call | tf_op jit(solution)/shard_map/pallas_call | solution.py:218
  2.0 7.4 %all-to-all-start = ((bf16[16,56,128]{2,1,0:T(8,128)(2,1)}), bf16[16,56,128]{2,1,0:T(8,128)(2,1)S(1)}, u32[]{:S(2)}, u32[]{:S(2)}) async-start(bf16[16,56,128]{2,1,0:T(8,128)(2,1)} %bitcast.19), calls=%async_computation | async-start | bytes 458752 | tf_op jit(solution)/shard_map/all_to_all | solution.py:234
  9.5 0.0 copy-done.6
  9.5 0.0 copy-start.3
  9.5 0.1 copy.15
  9.6 0.0 copy-start.4
  9.6 0.0 copy-start.5
  9.6 0.6 %copy-done.3 = bf16[64,64]{1,0:T(8,128)(2,1)S(1)} copy-done((bf16[64,64]{1,0:T(8,128)(2,1)S(1)}, bf16[64,64]{1,0:T(8,128)(2,1)}, u32[]{:S(2)}) %copy-start.3) | copy-done | bytes 8216
  10.2 0.1 copy-done.4
  10.3 0.0 copy-done.5
  10.3 0.0 copy-start.7
  10.3 0.0 copy-start
  10.3 0.0 copy-start.1
  10.3 0.0 copy-start.2
  10.3 0.9 %shard_map.119 = (bf16[1024,256]{1,0:T(8,128)(2,1)S(1)}, f32[32,128]{1,0:T(8,128)S(1)}) custom-call(bf16[64,64]{1,0:T(8,128)(2,1)S(1)} %copy-done.3, bf16[32,64]{1,0:T(8,128)(2,1)S(1)} %bitcast.17, bf16[32,32,128]{2,1,0:T(8,128)(2,1)S(1)} %bitcast.15, s32[8]{0:T(128)S(1)} %copy-done.5, s32[1]{0:T(128)} %bitcast.8.device_ref), custom_call_target="tpu_custom_call" | custom-call | tf_op jit(solution)/shard_map/pallas_call | solution.py:237
  11.3 0.0 copy-done.7
  11.3 7.7 %all-to-all-done = bf16[16,56,128]{2,1,0:T(8,128)(2,1)S(1)} async-done(((bf16[16,56,128]{2,1,0:T(8,128)(2,1)}), bf16[16,56,128]{2,1,0:T(8,128)(2,1)S(1)}, u32[]{:S(2)}, u32[]{:S(2)}) %all-to-all-start) | async-done | bytes 229408 | tf_op jit(solution)/shard_map/all_to_all | solution.py:234
  18.9 0.0 copy-done
  18.9 0.0 copy-done.1
  18.9 0.0 copy-done.2
  18.9 1.3 %shard_map.120 = bf16[64,128]{1,0:T(8,128)(2,1)} custom-call(bf16[896,128]{1,0:T(8,128)(2,1)S(1)} %bitcast.16, bf16[1024,256]{1,0:T(8,128)(2,1)S(1)} %get-tuple-element.11.folded_ref, f32[32,128]{1,0:T(8,128)S(1)} %get-tuple-element.12.same_ref, f32[1,128]{1,0:T(1,128)S(1)} %bitcast_convert_fusion.offset_ref, bf16[64,128]{1,0:T(8,128)(2,1)S(1)} %copy-done.2, ...), custom_call_target="tpu_custom_call" | custom-call | tf_op jit(solution)/shard_map/pallas_call | solution.py:257
  (1 shorter events, 0.0 us)
Async XLA Ops:
  0.0 9.5 %copy-start.6 = (bf16[1024,128]{1,0:T(8,128)(2,1)S(1)}, bf16[1024,128]{1,0:T(8,128)(2,1)}, u32[]{:S(2)}) copy-start(bf16[1024,128]{1,0:T(8,128)(2,1)} %param.15) | copy-start | bytes 786436
  2.0 16.9 %all-to-all-start = ((bf16[16,56,128]{2,1,0:T(8,128)(2,1)}), bf16[16,56,128]{2,1,0:T(8,128)(2,1)S(1)}, u32[]{:S(2)}, u32[]{:S(2)}) async-start(bf16[16,56,128]{2,1,0:T(8,128)(2,1)} %bitcast.19), calls=%async_computation | async-start | bytes 458752 | tf_op jit(solution)/shard_map/all_to_all | solution.py:234
  9.5 0.7 %copy-start.3 = (bf16[64,64]{1,0:T(8,128)(2,1)S(1)}, bf16[64,64]{1,0:T(8,128)(2,1)}, u32[]{:S(2)}) copy-start(bf16[64,64]{1,0:T(8,128)(2,1)} %get-tuple-element.10.normed_ref) | copy-start | bytes 24580
  9.6 0.7 %copy-start.4 = (bf16[64,32]{0,1:T(8,128)(2,1)S(1)}, bf16[64,32]{0,1:T(8,128)(2,1)}, u32[]{:S(2)}) copy-start(bf16[64,32]{0,1:T(8,128)(2,1)} %param.13) | copy-start | bytes 12292
  9.6 0.7 %copy-start.5 = (s32[8]{0:T(128)S(1)}, s32[8]{0:T(128)}, u32[]{:S(2)}) copy-start(s32[8]{0:T(128)} %lengths_ref.1) | copy-start | bytes 100
  10.3 1.0 %copy-start.7 = (bf16[128]{0:T(256)(128)(2,1)S(1)}, bf16[128]{0:T(256)(128)(2,1)}, u32[]{:S(2)}) copy-start(bf16[128]{0:T(256)(128)(2,1)} %param.16) | copy-start | bytes 772
  10.3 8.6 %copy-start = (bf16[128,128]{1,0:T(8,128)(2,1)S(1)}, bf16[128,128]{1,0:T(8,128)(2,1)}, u32[]{:S(2)}) copy-start(bf16[128,128]{1,0:T(8,128)(2,1)} %sigmoid_ref.1) | copy-start | bytes 98308
  10.3 8.6 %copy-start.1 = (bf16[128,128]{1,0:T(8,128)(2,1)S(1)}, bf16[128,128]{1,0:T(8,128)(2,1)}, u32[]{:S(2)}) copy-start(bf16[128,128]{1,0:T(8,128)(2,1)} %content_ref.1) | copy-start | bytes 98308
  10.3 8.6 %copy-start.2 = (bf16[64,128]{1,0:T(8,128)(2,1)S(1)}, bf16[64,128]{1,0:T(8,128)(2,1)}, u32[]{:S(2)}) copy-start(bf16[64,128]{1,0:T(8,128)(2,1)} %structural_ref.1) | copy-start | bytes 49156

commit v3 on v2

--- a/solution.py
+++ b/solution.py
@@ -10,7 +10,6 @@
 
 CAP = 2
 LANES = 128
-CODE_ROWS = 8
 VMEM = pltpu.MemorySpace.VMEM
 SMEM = pltpu.MemorySpace.SMEM
 
@@ -29,12 +28,61 @@
     return centred * lax.rsqrt(variance + 1e-05)
 
 
-def pack_kernel(n_devices, rows, x_ref, second_ref, tiles_ref, owner_ref, column_ref, send_ref, normed_ref, wide):
+def pack_kernel(
+    n_devices,
+    rows,
+    x_hbm,
+    second_hbm,
+    tiles_hbm,
+    owner_hbm,
+    column_hbm,
+    send_ref,
+    normed_ref,
+    x_ref,
+    second_ref,
+    tiles_ref,
+    owner_ref,
+    column_ref,
+    wide,
+    arrived,
+):
+    loads = [
+        pltpu.make_async_copy(source, target, arrived.at[n])
+        for n, (source, target) in enumerate(
+            (
+                (owner_hbm, owner_ref),
+                (column_hbm, column_ref),
+                (x_hbm, x_ref),
+                (second_hbm, second_ref),
+                (tiles_hbm, tiles_ref),
+            )
+        )
+    ]
+    for load in loads:
+        load.start()
     depth, lines, _ = x_ref.shape
     slots, width = tiles_ref.shape
     tile_rows = width // LANES
     n_chan = second_ref.shape[0]
     right_rows = n_chan * depth // LANES
+    base = lines * right_rows
+    here = lax.broadcasted_iota(jnp.int32, (slots, slots), 0)
+    there = lax.broadcasted_iota(jnp.int32, (slots, slots), 1)
+    for load in loads[:2]:
+        load.wait()
+    across = jnp.broadcast_to(owner_ref[...], (slots, slots))
+    down = jnp.sum(jnp.where(here == there, across, 0), axis=1, keepdims=True)
+    rank = jnp.sum(jnp.where((down == across) & (here < there), 1, 0), axis=0, keepdims=True)
+    target = rank * n_devices + owner_ref[...]
+    place = lax.broadcasted_iota(jnp.int32, (CAP * n_devices, slots), 0) == target
+    code = jnp.where(place, (column_ref[...] + 1).astype(jnp.float32), 0.0)
+    code = jnp.broadcast_to(jnp.sum(code, axis=1, keepdims=True), (CAP * n_devices, LANES))
+    for c in range(CAP):
+        wide[pl.ds(base + CAP * tile_rows + c, n_devices, stride=rows), :] = code[
+            c * n_devices : (c + 1) * n_devices
+        ]
+    for load in loads[2:]:
+        load.wait()
     x = x_ref[...].astype(jnp.float32)
     for t in range(lines):
         normed = standardize(x[:, t, :]).astype(jnp.bfloat16)
@@ -46,18 +94,6 @@
         )
         for d in range(n_devices):
             wide[pl.ds(d * rows + t * right_rows, right_rows), :] = packed
-    owner = owner_ref[...]
-    here = lax.broadcasted_iota(jnp.int32, (slots, slots), 0)
-    there = lax.broadcasted_iota(jnp.int32, (slots, slots), 1)
-    across = jnp.broadcast_to(owner, (slots, slots))
-    down = jnp.sum(jnp.where(here == there, across, 0), axis=1, keepdims=True)
-    rank = jnp.sum(jnp.where((down == across) & (here < there), 1, 0), axis=0, keepdims=True)
-    target = rank * n_devices + owner
-    place = lax.broadcasted_iota(jnp.int32, (CAP * n_devices, slots), 0) == target
-    base = lines * right_rows
-    code = jnp.where(place, (column_ref[...] + 1).astype(jnp.float32), 0.0)
-    code = jnp.sum(code, axis=1, keepdims=True)
-    code = jnp.broadcast_to(code, (CAP * n_devices, LANES))
     place = place.astype(jnp.bfloat16)
     for q in range(tile_rows):
         placed = dot(place, tiles_ref[:, q * LANES : (q + 1) * LANES])
@@ -65,10 +101,6 @@
             wide[pl.ds(base + c * tile_rows + q, n_devices, stride=rows), :] = placed[
                 c * n_devices : (c + 1) * n_devices
             ]
-    base = base + CAP * tile_rows
-    for c in range(CODE_ROWS):
-        piece = min(c, CAP - 1)
-        wide[pl.ds(base + c, n_devices, stride=rows), :] = code[piece * n_devices : (piece + 1) * n_devices]
     send_ref[...] = wide[...].astype(jnp.bfloat16)
 
 
@@ -119,65 +151,87 @@
     sigmoid_ref,
     content_ref,
     out_ref,
-    right_wide,
+    wide,
     sums,
     pair,
+    final,
 ):
     n_temp, pair_chan = structural_ref.shape
     lines = folded_ref.shape[1] // pair_chan
-    depth_chan = folded_ref.shape[0]
-    right_rows = depth_chan // LANES
+    right_rows = folded_ref.shape[0] // LANES
     n_tokens = n_devices * lines
-    height = same_ref.shape[0]
     n_tiles = n_tokens // tc
-    tile_rows = height // n_tiles
+    tile_rows = same_ref.shape[0] // n_tiles
     base = lines * right_rows
-    code_base = base + CAP * tile_rows
-
-    sums[...] = jnp.zeros_like(sums)
+    wide[...] = got_ref[...].astype(jnp.float32)
+
+    unrolled = n_devices <= 16
+    if not unrolled:
+        sums[...] = jnp.zeros_like(sums)
 
     def add_source(d, carry):
-        start = pl.multiple_of(d * rows, 8)
-        right_wide[pl.ds(pl.multiple_of(d * base, 8), base), :] = got_ref[pl.ds(start, base), :].astype(
-            jnp.float32
-        )
-        codes = got_ref[pl.ds(start + code_base, CODE_ROWS), :].astype(jnp.float32)
-        counts = list(carry)
+        start = d * rows
+        counts, totals = carry
         for c in range(CAP):
-            tile = got_ref[pl.ds(start + base + c * tile_rows, tile_rows), :].astype(jnp.float32)
-            code = codes[c : c + 1, :]
+            tile = wide[pl.ds(start + base + c * tile_rows, tile_rows), :]
+            code = wide[pl.ds(start + base + CAP * tile_rows + c, 1), :]
             for k in range(n_tiles):
                 hit = code == k + 1.0
                 counts[k] = counts[k] + jnp.where(hit, 1.0, 0.0)
-                at = pl.ds(k * tile_rows, tile_rows)
-                sums[at, :] = sums[at, :] + jnp.where(hit, tile, 0.0)
-        return tuple(counts)
-
-    counts = tuple(jnp.zeros((1, LANES), jnp.float32) for _ in range(n_tiles))
-    counts = lax.fori_loop(0, n_devices, add_source, counts, unroll=n_devices <= 16)
+                term = jnp.where(hit, tile, 0.0)
+                if unrolled:
+                    totals[k] = term if totals[k] is None else totals[k] + term
+                else:
+                    at = pl.ds(k * tile_rows, tile_rows)
+                    sums[at, :] = sums[at, :] + term
+        return counts, totals
+
+    counts = [jnp.zeros((1, LANES), jnp.float32) for _ in range(n_tiles)]
+    totals = [None] * n_tiles
+    if unrolled:
+        for d in range(n_devices):
+            counts, totals = add_source(d, (counts, totals))
+    else:
+        counts = lax.fori_loop(0, n_devices, lambda d, kept: add_source(d, (kept, totals))[0], counts)
+        totals = [sums[pl.ds(k * tile_rows, tile_rows), :] for k in range(n_tiles)]
+    outer = None
+    for g in range(right_rows):
+        lhs = jnp.concatenate(
+            [wide[pl.ds(t * right_rows + g, n_devices, stride=rows), :] for t in range(lines)], axis=0
+        ).astype(jnp.bfloat16)
+        term = dot(lhs, folded_ref[pl.ds(g * LANES, LANES), :])
+        outer = term if outer is None else outer + term
+    packed = LANES // n_temp
+    per_row = tile_rows // lines
     for k in range(n_tiles):
         at = pl.ds(k * tile_rows, tile_rows)
-        mean = sums[at, :] / jnp.maximum(counts[k], 1.0)
+        mean = totals[k] / jnp.maximum(counts[k], 1.0)
         template = (mean * same_ref[at, :]).astype(jnp.bfloat16)
-        for h in range(LANES // n_temp):
+        for h in range(packed):
             part = dot(template[:, h * n_temp : (h + 1) * n_temp], structural_ref[...])
-            per_row = tile_rows // lines
-            for t in range(lines):
-                pair[pl.ds(t * n_tokens + k * tc + h, per_row, stride=LANES // n_temp), :] = part[
-                    t * per_row : (t + 1) * per_row
-                ]
-    outer = None
-    for g in range(right_rows):
-        lhs = right_wide[pl.ds(g, n_tokens, stride=right_rows), :].astype(jnp.bfloat16)
-        term = dot(lhs, folded_ref[pl.ds(g * LANES, LANES), :])
-        outer = term if outer is None else outer + term
-    for t in range(lines):
-        at = pl.ds(t * n_tokens, n_tokens)
-        total = pair[at, :] + (outer[:, t * pair_chan : (t + 1) * pair_chan] + offset_ref[...])
+            for i in range(lines):
+                if packed == lines:
+                    where = pl.ds(i * n_tokens + h * n_devices + k * per_row, per_row)
+                else:
+                    first = k * tc + h
+                    where = pl.ds(
+                        i * n_tokens + (first % lines) * n_devices + first // lines,
+                        per_row,
+                        stride=packed // lines,
+                    )
+                pair[where, :] = part[i * per_row : (i + 1) * per_row]
+    for i in range(lines):
+        at = pl.ds(i * n_tokens, n_tokens)
+        total = pair[at, :] + (outer[:, i * pair_chan : (i + 1) * pair_chan] + offset_ref[...])
         pair_normed = standardize(total).astype(jnp.bfloat16)
         gate = jax.nn.sigmoid(dot(pair_normed, sigmoid_ref[...]))
         linear = dot(pair_normed, content_ref[...])
-        out_ref[at, :] = (gate * linear).astype(out_ref.dtype)
+        result = gate * linear
+        for t in range(lines):
+            final[pl.ds(i * n_tokens + t, n_devices, stride=lines), :] = result[
+                t * n_devices : (t + 1) * n_devices
+            ]
+    out_ref[...] = final[...].astype(out_ref.dtype)
 
 
 def grant(*arrays):
@@ -211,9 +265,10 @@
     n_tiles = n_tokens // tc
     tile_rows = width // LANES
     right_rows = n_chan * depth // LANES
-    rows = lines * right_rows + CAP * tile_rows + CODE_ROWS
+    rows = lines * right_rows + CAP * tile_rows + CAP
     vmem = pl.BlockSpec(memory_space=VMEM)
     smem = pl.BlockSpec(memory_space=SMEM)
+    hbm = pl.BlockSpec(memory_space=pltpu.MemorySpace.HBM)
 
     send, normed = pl.pallas_call(
         functools.partial(pack_kernel, n_devices, rows),
@@ -221,9 +276,17 @@
             jax.ShapeDtypeStruct((n_devices * rows, LANES), jnp.bfloat16),
             jax.ShapeDtypeStruct((lines * depth, n_feat), jnp.bfloat16),
         ),
-        in_specs=[vmem] * 5,
+        in_specs=[hbm] * 5,
         out_specs=(vmem, vmem),
-        scratch_shapes=[pltpu.VMEM((n_devices * rows, LANES), jnp.float32)],
+        scratch_shapes=[
+            pltpu.VMEM(aligned_sequences.shape, jnp.bfloat16),
+            pltpu.VMEM((n_chan, n_feat), jnp.bfloat16),
+            pltpu.VMEM((slots, width), jnp.bfloat16),
+            pltpu.VMEM((1, slots), jnp.int32),
+            pltpu.VMEM((1, slots), jnp.int32),
+            pltpu.VMEM((n_devices * rows, LANES), jnp.float32),
+            pltpu.SemaphoreType.DMA((5,)),
+        ],
     )(
         aligned_sequences,
         second_factor_matrix.T,
@@ -232,7 +295,7 @@
         patch_target_index.reshape(1, slots),
     )
     got = lax.all_to_all(
-        send.reshape(n_devices, rows, LANES), "row", split_axis=0, concat_axis=0, tiled=True
+        send.reshape(n_devices, rows // 2, 2, LANES), "row", split_axis=0, concat_axis=0, tiled=True
     ).reshape(n_devices * rows, LANES)
     folded, same = pl.pallas_call(
         functools.partial(left_kernel, n_tiles, tc),
@@ -260,16 +323,17 @@
         in_specs=[vmem] * 7,
         out_specs=vmem,
         scratch_shapes=[
-            pltpu.VMEM((n_devices * lines * right_rows, LANES), jnp.float32),
+            pltpu.VMEM((n_devices * rows, LANES), jnp.float32),
             pltpu.VMEM((n_tiles * tile_rows, LANES), jnp.float32),
+            pltpu.VMEM((lines * n_tokens, pair_chan), jnp.float32),
             pltpu.VMEM((lines * n_tokens, pair_chan), jnp.float32),
         ],
         compiler_params=grant(
             ((n_devices * rows, LANES), jnp.bfloat16),
             ((n_chan * depth, lines * pair_chan), jnp.bfloat16),
-            ((n_devices * lines * right_rows, LANES), jnp.float32),
+            ((n_devices * rows, LANES), jnp.float32),
             ((2 * n_tiles * tile_rows, LANES), jnp.float32),
-            ((2 * lines * n_tokens, pair_chan), jnp.float32),
+            ((3 * lines * n_tokens, pair_chan), jnp.float32),
         ),
     )(
         got,

time: 20.6 us -> 20.3 us (0.985)
  waiting for transfers between devices: 7.65 us -> 7.25 us
    all_to_all x1, waiting for transfers between devices: 7.65 us -> 7.25 us  [on_device(): lax.all_to_all(send.reshape(n_devices, rows // 2, 2, LANES), 'row', split...]
where the time goes in v3:
time: 20.3 us; the launch traced here: 19.9 us
  starting transfers between devices  7.43 us (37%)
  waiting for transfers between devices  7.25 us (36%)
  Pallas kernels  4.32 us (21%)
  local copies, waits for them, and re-layouts  0.81 us (4%)
    all_to_all x1, starting transfers between devices, on_device(): lax.all_to_all(send.reshape(n_devices, rows // 2, 2, LANES), 'row', split...  7.43 us
    all_to_all x1, waiting for transfers between devices, on_device(): lax.all_to_all(send.reshape(n_devices, rows // 2, 2, LANES), 'row', split...  7.25 us
    pallas_call x1, Pallas kernels, on_device(): pl.pallas_call(functools.partial(pack_kernel, n_devices, rows), out_shape...  2.08 us
    pallas_call x1, Pallas kernels, on_device(): pl.pallas_call(functools.partial(pair_kernel, n_devices, rows, tc), out_s...  1.28 us
    pallas_call x1, Pallas kernels, on_device(): pl.pallas_call(functools.partial(left_kernel, n_tiles, tc), out_shape=(ja...  0.95 us
    unnamed x16, local copies, waits for them, and re-layouts  0.71 us
  transfers between devices with their start and end apart: 1, of which 1 were waited for; matrix products, arithmetic and copies ran while one was open for 1% of the time, Pallas kernels for 5%

profile of v3, /device:TPU:0, one launch (start us, length us, event | category | flops | bytes accessed | tf_op | source)
XLA Modules:
  0.0 19.9 jit_solution(17045292979128626012)
XLA Ops:
  0.0 0.0 copy-start.6
  0.0 2.1 %shard_map.118 = (bf16[800,128]{1,0:T(8,128)(2,1)}, bf16[64,64]{1,0:T(8,128)(2,1)}) custom-call(bf16[32,2,64]{2,1,0:T(2,128)(2,1)} %x_hbm.1, bf16[32,64]{1,0:T(8,128)(2,1)} %bitcast.20, bf16[16,2048]{1,0:T(8,128)(2,1)} %tiles_hbm.1, s32[1,16]{1,0:T(1,128)} %bitcast.21, s32[1,16]{1,0:T(1,128)} %bitcast.22), custom_call_target="tpu_custom_call" | custom-call | tf_op jit(solution)/shard_map/pallas_call | solution.py:273
  2.1 7.4 %all-to-all-start = ((bf16[16,25,2,128]{3,2,1,0:T(2,128)(2,1)}), bf16[16,25,2,128]{3,2,1,0:T(2,128)(2,1)S(1)}, u32[]{:S(2)}, u32[]{:S(2)}) async-start(bf16[16,25,2,128]{3,2,1,0:T(2,128)(2,1)} %bitcast.19), calls=%async_computation | async-start | bytes 409600 | tf_op jit(solution)/shard_map/all_to_all | solution.py:297
  9.5 0.0 copy-done.6
  9.5 0.0 copy-start.3
  9.6 0.1 copy.15
  9.7 0.0 copy-start.4
  9.7 0.0 copy-start.5
  9.7 0.6 %copy-done.3 = bf16[64,64]{1,0:T(8,128)(2,1)S(1)} copy-done((bf16[64,64]{1,0:T(8,128)(2,1)S(1)}, bf16[64,64]{1,0:T(8,128)(2,1)}, u32[]{:S(2)}) %copy-start.3) | copy-done | bytes 8216
  10.3 0.1 copy-done.4
  10.4 0.0 copy-done.5
  10.4 0.0 copy-start.7
  10.4 0.0 copy-start
  10.4 0.0 copy-start.1
  10.4 0.0 copy-start.2
  10.4 1.0 %shard_map.119 = (bf16[1024,256]{1,0:T(8,128)(2,1)S(1)}, f32[32,128]{1,0:T(8,128)S(1)}) custom-call(bf16[64,64]{1,0:T(8,128)(2,1)S(1)} %copy-done.3, bf16[32,64]{1,0:T(8,128)(2,1)S(1)} %bitcast.17, bf16[32,32,128]{2,1,0:T(8,128)(2,1)S(1)} %bitcast.15, s32[8]{0:T(128)S(1)} %copy-done.5, s32[1]{0:T(128)} %bitcast.8.device_ref), custom_call_target="tpu_custom_call" | custom-call | tf_op jit(solution)/shard_map/pallas_call | solution.py:300
  11.4 0.0 copy-done.7
  11.4 7.2 %all-to-all-done = bf16[16,25,2,128]{3,2,1,0:T(2,128)(2,1)S(1)} async-done(((bf16[16,25,2,128]{3,2,1,0:T(2,128)(2,1)}), bf16[16,25,2,128]{3,2,1,0:T(2,128)(2,1)S(1)}, u32[]{:S(2)}, u32[]{:S(2)}) %all-to-all-start) | async-done | bytes 204832 | tf_op jit(solution)/shard_map/all_to_all | solution.py:297
  18.6 0.0 copy-done
  18.6 0.0 copy-done.1
  18.6 0.0 copy-done.2
  18.6 1.3 %shard_map.120 = bf16[64,128]{1,0:T(8,128)(2,1)} custom-call(bf16[800,128]{1,0:T(8,128)(2,1)S(1)} %bitcast.16, bf16[1024,256]{1,0:T(8,128)(2,1)S(1)} %get-tuple-element.11.folded_ref, f32[32,128]{1,0:T(8,128)S(1)} %get-tuple-element.12.same_ref, f32[1,128]{1,0:T(1,128)S(1)} %bitcast_convert_fusion.offset_ref, bf16[64,128]{1,0:T(8,128)(2,1)S(1)} %copy-done.2, ...), custom_call_target="tpu_custom_call" | custom-call | tf_op jit(solution)/shard_map/pallas_call | solution.py:320
  (1 shorter events, 0.0 us)
Async XLA Ops:
  0.0 9.5 %copy-start.6 = (bf16[1024,128]{1,0:T(8,128)(2,1)S(1)}, bf16[1024,128]{1,0:T(8,128)(2,1)}, u32[]{:S(2)}) copy-start(bf16[1024,128]{1,0:T(8,128)(2,1)} %param.15) | copy-start | bytes 786436
  2.1 16.5 %all-to-all-start = ((bf16[16,25,2,128]{3,2,1,0:T(2,128)(2,1)}), bf16[16,25,2,128]{3,2,1,0:T(2,128)(2,1)S(1)}, u32[]{:S(2)}, u32[]{:S(2)}) async-start(bf16[16,25,2,128]{3,2,1,0:T(2,128)(2,1)} %bitcast.19), calls=%async_computation | async-start | bytes 409600 | tf_op jit(solution)/shard_map/all_to_all | solution.py:297
  9.5 0.7 %copy-start.3 = (bf16[64,64]{1,0:T(8,128)(2,1)S(1)}, bf16[64,64]{1,0:T(8,128)(2,1)}, u32[]{:S(2)}) copy-start(bf16[64,64]{1,0:T(8,128)(2,1)} %get-tuple-element.10.normed_ref) | copy-start | bytes 24580
  9.7 0.7 %copy-start.4 = (bf16[64,32]{0,1:T(8,128)(2,1)S(1)}, bf16[64,32]{0,1:T(8,128)(2,1)}, u32[]{:S(2)}) copy-start(bf16[64,32]{0,1:T(8,128)(2,1)} %param.13) | copy-start | bytes 12292
  9.7 0.7 %copy-start.5 = (s32[8]{0:T(128)S(1)}, s32[8]{0:T(128)}, u32[]{:S(2)}) copy-start(s32[8]{0:T(128)} %lengths_ref.1) | copy-start | bytes 100
  10.4 1.0 %copy-start.7 = (bf16[128]{0:T(256)(128)(2,1)S(1)}, bf16[128]{0:T(256)(128)(2,1)}, u32[]{:S(2)}) copy-start(bf16[128]{0:T(256)(128)(2,1)} %param.16) | copy-start | bytes 772
  10.4 8.3 %copy-start = (bf16[128,128]{1,0:T(8,128)(2,1)S(1)}, bf16[128,128]{1,0:T(8,128)(2,1)}, u32[]{:S(2)}) copy-start(bf16[128,128]{1,0:T(8,128)(2,1)} %sigmoid_ref.1) | copy-start | bytes 98308
  10.4 8.3 %copy-start.1 = (bf16[128,128]{1,0:T(8,128)(2,1)S(1)}, bf16[128,128]{1,0:T(8,128)(2,1)}, u32[]{:S(2)}) copy-start(bf16[128,128]{1,0:T(8,128)(2,1)} %content_ref.1) | copy-start | bytes 98308
  10.4 8.2 %copy-start.2 = (bf16[64,128]{1,0:T(8,128)(2,1)S(1)}, bf16[64,128]{1,0:T(8,128)(2,1)}, u32[]{:S(2)}) copy-start(bf16[64,128]{1,0:T(8,128)(2,1)} %structural_ref.1) | copy-start | bytes 49156
